TPU v7x, 256 devices: a whole 4x4x8 slice. The times are simulated.
256 devices in a mesh: grid: 8 (over x_lo, y), dom: 32 (over z, x_hi, core).
Axes of the slice: x: 4 (x_hi: 2, x_lo: 2; x = x_hi * 2 + x_lo), y: 4, z: 8, core: 2. Of those that a mesh axis runs over, the one named last changes fastest.
Arguments:
- state_field: float32 [8, 64, 8, 16384], P('grid', 'dom'), may hold values from -6 to 6
- level_vectors: int32 [8, 4], P('grid'), may hold values from 2 to 5, as said below
- combine_weights: int32 [8], P('grid'), may hold values from -2 to 2, as said below
- diffusion: float32 [6], replicated, may hold values from 0.05 to 0.08
- courant: float32 [6], replicated, may hold values from -0.3 to 0.3
Outputs:
- combined_field: float32 [8, 64, 8, 16384], P('grid', 'dom')
Inputs may be any that keep to these rules, and one draw needn't show every extreme that they name: `level_vectors`: each row holds 2, 3, 4, 5 in some order. `combine_weights`: never zero.
All inputs are finite; a program needn't handle non-finite values.
Results may differ from a plain program's by a relative error of at most 0.0003.
Values sent between devices are 32-bit elements; how exact they have to be, the bound alone decides.
No kernel may reach another device: no remote copies, remote signals or barrier semaphores. Data moves between devices by JAX's collectives and lax.ppermute only.
A program may use at most 128 MiB of HBM per device.

v0:
```python
import jax
import jax.numpy as jnp
from jax import lax
from jax.experimental import pallas as pl
from jax.experimental.pallas import tpu as pltpu
from jax.sharding import PartitionSpec as P

VMEM = pltpu.VMEM
SMEM = pltpu.SMEM
F32 = jnp.float32
BF16 = jnp.bfloat16
LANES = 128
COLS = 16384
MORE = 8192


def roll(x, shift, axis):
    return pltpu.roll(x, shift, axis)


def numbers(level_ref, diff_ref, cour_ref):
    kappa = [diff_ref[0], diff_ref[1]]
    sigma = [cour_ref[0], cour_ref[1]]
    for j in range(4):
        k, s = F32(0.0), F32(0.0)
        for p in range(4):
            hit = level_ref[0, p] == 2 + j
            k = jnp.where(hit, diff_ref[2 + p], k)
            s = jnp.where(hit, cour_ref[2 + p], s)
        kappa.append(k)
        sigma.append(s)
    fwd = [k - 0.5 * s for k, s in zip(kappa, sigma)]
    bwd = [k + 0.5 * s for k, s in zip(kappa, sigma)]
    centre = 1.0 - 2.0 * (kappa[0] + kappa[1] + kappa[2] + kappa[3] + kappa[4] + kappa[5])
    return fwd, bwd, centre


def parity():
    return lax.axis_index("dom") % 2


def across_layers():
    d = lax.axis_index("dom") % 4
    return (d == 0) | (d == 3)


def sides(fwd, bwd, p):
    off = jnp.where(p == 0, bwd[0], fwd[0])
    core = jnp.where(p == 0, fwd[0], bwd[0])
    return off, core


BAND = 4096


def band(ref, i2):
    start = pl.multiple_of(i2 * BAND, BAND)
    return ref.at[:, pl.ds(start, BAND)]


def chunk(d3, c4):
    start = (d3 * 4 + c4) * LANES
    return slice(start, start + LANES)


def stencil(source, prepare, finish, i2, nums):
    fwd, bwd, centre = nums
    lane = lanes()
    inner = lane % 32
    not_top, not_low = lane < 96, lane >= 32
    first, last = inner == 0, inner == 31
    here, above, below = band(source, i2), band(source, (i2 + 1) % 4), band(source, (i2 + 3) % 4)
    group = lambda ref, d3: [ref[:, chunk(d3 % 8, c)] for c in range(4)]
    low, v = group(here, 7), group(here, 0)
    waiting = None
    for d3 in range(8):
        high, over, under = group(here, d3 + 1), group(above, d3), group(below, d3)
        beside = [prepare(chunk(d3, c)) for c in range(4)]
        ahead = [roll(x, 96, 1) for x in v]
        behind = [roll(x, 32, 1) for x in v]
        done = []
        for c in range(4):
            x = v[c]
            total = centre * x
            total += fwd[1] * roll(x, 7, 0) + bwd[1] * roll(x, 1, 0)
            total += fwd[2] * over[c] + bwd[2] * under[c]
            total += fwd[3] * high[c] + bwd[3] * low[c]
            total += fwd[4] * jnp.where(not_top, ahead[c], ahead[(c + 1) % 4])
            total += bwd[4] * jnp.where(not_low, behind[c], behind[(c + 3) % 4])
            total += fwd[5] * roll(jnp.where(first, behind[c], x), 127, 1)
            total += bwd[5] * roll(jnp.where(last, ahead[c], x), 1, 1)
            done.append(total)
        if waiting is not None:
            for item in waiting:
                finish(*item)
        waiting = [(chunk(d3, c), done[c], beside[c]) for c in range(4)]
        low, v = v, high
    for item in waiting:
        finish(*item)


def stream(i2, out, rule, *sources):
    out = band(out, i2)
    sources = [band(x, i2) for x in sources]
    for i in range(0, 32, 8):
        places = [slice((i + j) * LANES, (i + j + 1) * LANES) for j in range(8)]
        values = [rule(*[x[:, s] for x in sources]) for s in places]
        for s, value in zip(places, values):
            out[:, s] = value


def lanes():
    return lax.broadcasted_iota(jnp.int32, (8, LANES), 1)


def spots():
    for v in range(2):
        for i4 in range(4):
            for j in range(8):
                yield v, j, 2 * v + j % 2, j // 2, i4


def pack(load):
    code = lanes() // 32 * 8 + lanes() % 8
    out = [None, None]
    for v, j, i2, i3, i4 in spots():
        start = i2 * BAND + (i3 * 8 + i4) * LANES
        x = load(slice(start, start + LANES))
        shift = 32 * i4 + j
        x = roll(x, shift, 1) if shift else x
        out[v] = x if out[v] is None else jnp.where(code == 8 * i4 + j, x, out[v])
    return jnp.concatenate(out, axis=1)


def first_kernel(
    u_ref, level_ref, diff_ref, cour_ref, weight_ref, head_ref, tail_ref, z_ref, off_ref, scale_ref, sems
):
    p = parity()
    x_ref, y_ref = u_ref.at[p], u_ref.at[1 - p]
    moves = [
        (u_ref.at[p], head_ref.at[:, pl.ds(0, COLS)]),
        (u_ref.at[1 - p, :, pl.ds(0, MORE)], head_ref.at[:, pl.ds(COLS, MORE)]),
        (u_ref.at[1 - p, :, pl.ds(MORE, COLS - MORE)], tail_ref),
    ]
    copies = [pltpu.make_async_copy(source, target, sems.at[i]) for i, (source, target) in enumerate(moves)]
    for copy in copies:
        copy.start()
    nums = numbers(level_ref, diff_ref, cour_ref)
    fwd, bwd, _ = nums
    s_off, s_core = sides(fwd, bwd, p)
    for r, (own, other, factor) in enumerate(((x_ref, y_ref, 2.0 * s_core), (y_ref, x_ref, 2.0 * s_off))):

        def body(i2, carry):
            beside, out = band(other, i2), band(z_ref.at[r], i2)

            def finish(s, value, extra):
                out[:, s] = value + factor * extra

            stencil(own, lambda s: beside[:, s], finish, i2, nums)
            return carry

        lax.fori_loop(0, 4, body, 0)
    square, double = s_core * s_core, 2.0 * s_core
    off_ref[0:8, :] = pack(lambda s: double * z_ref[0, :, s] - (3.0 * square) * y_ref[:, s])
    off_ref[8:16, :] = square * pack(lambda s: x_ref[:, s])
    scale_ref[...] = jnp.full(scale_ref.shape, weight_ref[0].astype(F32))
    for copy in copies:
        copy.wait()


def storage_index(packed):
    i2 = (packed >> 7) * 2 + (packed & 1)
    return i2 * 64 + ((packed >> 1) & 3) * 16 + ((packed >> 5) & 3) * 4 + ((packed >> 3) & 3)


def point_table(level_ref):
    rows = storage_index(lax.broadcasted_iota(jnp.int32, (256, LANES), 0))
    physical = jnp.zeros((256, LANES), jnp.int32)
    for p in range(4):
        stored = level_ref[0, p] - 2
        physical = physical | (((rows >> (2 * (3 - stored))) & 3) << (2 * (3 - p)))
    halves = []
    for half in range(2):
        cols = storage_index(lax.broadcasted_iota(jnp.int32, (8, LANES), 1) + half * LANES)
        halves.append(jnp.where(physical == cols[0:1], 1.0, 0.0))
    return jnp.concatenate(halves, axis=1).astype(BF16)


def exact_dot(x, table, across):
    high = x.astype(BF16)
    rest = x - high.astype(F32)
    middle = rest.astype(BF16)
    low = (rest - middle.astype(F32)).astype(BF16)
    dims = (((1,), (1 if across else 0,)), ((), ()))
    parts = jnp.concatenate([high, middle, low], axis=0)
    done = lax.dot_general(parts, table, dims, preferred_element_type=F32)
    n = x.shape[0]
    return done[:n] + (done[n : 2 * n] + done[2 * n :])


def second_kernel(
    u_ref,
    z_ref,
    k_ref,
    off_ref,
    level_ref,
    diff_ref,
    cour_ref,
    scale_ref,
    acc_ref,
    full_ref,
    own_ref,
    t_ref,
    map_ref,
):
    nums = numbers(level_ref, diff_ref, cour_ref)
    fwd, bwd, _ = nums
    p = parity()
    q = 1 - p
    _, s_core = sides(fwd, bwd, p)
    twice = 2.0 * fwd[0] * bwd[0]
    square, double = s_core * s_core, 2.0 * s_core

    def add(i2, carry):
        stream(i2, full_ref.at[1], lambda a, b: a + double * b, z_ref.at[1], k_ref.at[p])
        return carry

    lax.fori_loop(0, 4, add, 0)
    for r, (own, core) in enumerate(((u_ref.at[p], p), (u_ref.at[q], q))):

        def body(i2, carry):
            here, there, out = band(own, i2), band(k_ref.at[core], i2), band(acc_ref.at[r], i2)

            def finish(s, value, extra):
                out[:, s] = value + extra

            stencil(full_ref.at[r], lambda s: twice * here[:, s] + square * there[:, s], finish, i2, nums)
            return carry

        lax.fori_loop(0, 4, body, 0)
    own_ref[0:8, :] = pack(lambda s: acc_ref[0, :, s])
    own_ref[8:16, :] = pack(lambda s: acc_ref[1, :, s])
    table = point_table(level_ref)
    map_ref[...] = table
    weight = scale_ref[0:1, 0:1]
    both = jnp.concatenate([own_ref[...], off_ref[...]], axis=0)
    t_ref[...] = weight * exact_dot(both, table, False)


def gather_kernel(t_ref, a_ref, b_ref, c_ref, off_ref, far_ref, cross_ref, own_ref):
    total = (t_ref[...] + a_ref[...]) + (b_ref[...] + c_ref[...])
    own_ref[...] = total[0:16]
    cross_ref[...] = total[16:32]
    far_ref[0:16, :] = total[16:32]
    far_ref[16:32, :] = off_ref[...]


def near_kernel(acc_ref, zones_ref, same_ref, level_ref, diff_ref, cour_ref, out_ref, near_ref):
    nums = numbers(level_ref, diff_ref, cour_ref)
    fwd, bwd, _ = nums
    p = parity()
    layers = across_layers()
    s_off, _ = sides(fwd, bwd, p)
    square, double = s_off * s_off, 2.0 * s_off

    def gather(i2, carry):
        stream(i2, near_ref, lambda a, b: jnp.where(layers, a, b), zones_ref.at[1 - p], same_ref)
        return carry

    lax.fori_loop(0, 4, gather, 0)

    def body(i2, carry):
        near = band(near_ref, i2)
        old = [band(acc_ref.at[r], i2) for r in range(2)]
        new = [band(out_ref.at[r], i2) for r in range(2)]

        def prepare(s):
            return old[0][:, s], old[1][:, s] + square * near[:, s]

        def finish(s, value, extra):
            new[0][:, s] = extra[0] + double * value
            new[1][:, s] = extra[1]

        stencil(near_ref, prepare, finish, i2, nums)
        return carry

    lax.fori_loop(0, 4, body, 0)


def far_square(diff_ref, cour_ref, p):
    fwd = [diff_ref[0] - 0.5 * cour_ref[0]]
    bwd = [diff_ref[0] + 0.5 * cour_ref[0]]
    s_off, _ = sides(fwd, bwd, p)
    return s_off * s_off


def change_kernel(
    acc_ref,
    own_ref,
    sum_ref,
    far_ref,
    cross_ref,
    flip_ref,
    map_ref,
    zones_ref,
    head_ref,
    diff_ref,
    cour_ref,
    out_ref,
    rest_ref,
    chunks_ref,
    wide_ref,
    x_ref,
    y_ref,
    sems,
):
    p = parity()
    square = far_square(diff_ref, cour_ref, p)
    layers = across_layers()
    late_square = jnp.where(layers, square, 0.0)
    total = (sum_ref[...] + flip_ref[...]) + (far_ref[0:16, :] + cross_ref[...])
    own = own_ref[...] + far_ref[16:32, :]
    change = exact_dot(total, map_ref[...], True) - own
    for v, j, i2, i3, i4 in spots():
        k = (i2 * 4 + i3) * 4 + i4
        x = change[:, v * LANES : (v + 1) * LANES]
        shift = 32 * i4 + j
        chunks_ref[k * 16 : (k + 1) * 16, :] = roll(x, LANES - shift, 1) if shift else x
    source = lax.broadcasted_iota(jnp.int32, (LANES, 256), 0)
    target = lax.broadcasted_iota(jnp.int32, (LANES, 256), 1)
    lane = target % LANES
    step = lane // 32
    near = jnp.where(target < LANES, 4 - step, step)
    gap = (lane % 32 - source + 32) % 32
    reach = 8 - jnp.minimum(gap, 32 - gap)
    point = (source % 8 == 0) & (source < 32) & (reach > 0)
    table = jnp.where(point, (near * reach).astype(F32) * (1.0 / 32.0), 0.0).astype(BF16)
    wide_ref[...] = exact_dot(chunks_ref[...], table, False)
    copies = []
    for i2 in range(4):
        for c in range(4):
            planes = []
            for i3 in range(4):
                k, m = (i2 * 16 + i3 * 4 + c) * 16, (i2 * 16 + i3 * 4 + (c + 1) % 4) * 16
                planes.append(wide_ref[k : k + 16, 0:LANES] + wide_ref[m : m + 16, LANES:256])
            for d3 in range(8):
                value = planes[d3 // 2]
                if d3 % 2:
                    value = 0.5 * (value + planes[(d3 // 2 + 1) % 4])
                start = i2 * BAND + (d3 * 4 + c) * LANES
                s = slice(start, start + LANES)
                ready = acc_ref[0, :, s] + value[0:8]
                if start < MORE:
                    far = jnp.where(layers, zones_ref[p, :, s], head_ref[:, COLS + start : COLS + start + LANES])
                    x_ref[:, s] = ready + square * far
                else:
                    rest_ref[:, start - MORE : start - MORE + LANES] = ready + late_square * zones_ref[p, :, s]
                y_ref[:, s] = acc_ref[1, :, s] + value[8:16]
        s = pl.ds(i2 * BAND, BAND)
        copies.append(pltpu.make_async_copy(y_ref.at[:, s], out_ref.at[1 - p, :, s], sems.at[len(copies)]))
        copies[-1].start()
        if i2 * BAND < MORE:
            copies.append(pltpu.make_async_copy(x_ref.at[:, s], out_ref.at[p, :, s], sems.at[len(copies)]))
            copies[-1].start()
    late = pltpu.make_async_copy(rest_ref, out_ref.at[p, :, pl.ds(MORE, COLS - MORE)], sems.at[7])

    @pl.when(layers)
    def _():
        late.start()
        late.wait()

    for copy in copies:
        copy.wait()


PARTS = 2


def last_kernel(rest_ref, tail_ref, diff_ref, cour_ref, old_ref, out_ref, row_ref, sems):
    p = parity()
    square = far_square(diff_ref, cour_ref, p)
    width = (COLS - MORE) // PARTS

    @pl.when(jnp.logical_not(across_layers()))
    def _():
        copies = []
        for i in range(PARTS):
            s = slice(i * width, (i + 1) * width)
            row_ref[:, s] = rest_ref[:, s] + square * tail_ref[:, s]
            copy = pltpu.make_async_copy(
                row_ref.at[:, s], out_ref.at[p, :, pl.ds(MORE + s.start, width)], sems.at[i]
            )
            copy.start()
            copies.append(copy)
        for copy in copies:
            copy.wait()


def call(kernel, outs, spaces, scratch=(), aliases=None, space=VMEM):
    return pl.pallas_call(
        kernel,
        out_shape=[jax.ShapeDtypeStruct(s, d) for s, d in outs],
        in_specs=[pl.BlockSpec(memory_space=m) for m in spaces],
        out_specs=[pl.BlockSpec(memory_space=space if i == 0 else VMEM) for i in range(len(outs))],
        scratch_shapes=list(scratch),
        input_output_aliases=aliases or {},
        compiler_params=pltpu.CompilerParams(vmem_limit_bytes=24 * 2**20),
        cost_estimate=pl.CostEstimate(flops=1000, bytes_accessed=1000, transcendentals=0),
    )


def whole(state_field, level_vectors, combine_weights, diffusion, courant):
    u = state_field[0]
    shape = u.shape
    grids, doms = lax.axis_size("grid"), lax.axis_size("dom")
    pairs_same, pairs_zone = [], []
    for d in range(doms):
        right = (d + 1) % doms
        if d % 2:
            (pairs_same if d % 4 == 1 else pairs_zone).extend([(d, right), (right, d)])
    pairs_off = pairs_same + pairs_zone
    pairs_core = [(d, d ^ 1) for d in range(doms)]
    half = grids // 2
    pairs_flip = [(g, (g + half) % grids) for g in range(grids)]
    pairs_cross = [(g * doms + s, (g + half) % grids * doms + t) for g in range(grids) for s, t in pairs_off]

    numbers_in = (level_vectors, diffusion, courant)
    row, points, rest = (shape[1], shape[2]), (16, 256), (8, COLS - MORE)
    cores = lax.ppermute(u, "dom", pairs_core)
    zones = lax.ppermute(u, "dom", pairs_zone)
    head, tail, z, off, scale = call(
        first_kernel,
        [((8, COLS + MORE), F32), (rest, F32), (shape, F32), (points, F32), ((8, LANES), F32)],
        [VMEM] + [SMEM] * 4,
        scratch=[pltpu.SemaphoreType.DMA((3,))],
    )(u, *numbers_in, combine_weights)
    same_head = lax.ppermute(head, "dom", pairs_same)
    acc, _, own, t, table = call(
        second_kernel,
        [(shape, F32), (shape, F32), (points, F32), ((32, 256), F32), ((256, 256), BF16)],
        [VMEM] * 4 + [SMEM] * 3 + [VMEM],
        aliases={1: 1},
    )(u, z, cores, off, *numbers_in, scale)
    turned = []
    for k in range(1, half):
        pairs = [(g, g // half * half + (g + k) % half) for g in range(grids)]
        turned.append(lax.ppermute(t, "grid", pairs))
    far, cross, total = call(gather_kernel, [((32, 256), F32), (points, F32), (points, F32)], [VMEM] * 5)(
        t, *turned, off
    )
    far_in = lax.ppermute(far, "dom", pairs_off)
    cross_in = lax.ppermute(cross, ("grid", "dom"), pairs_cross)
    flip_in = lax.ppermute(total, "grid", pairs_flip)
    same_tail = lax.ppermute(tail, "dom", pairs_same)
    (acc,) = call(
        near_kernel,
        [(shape, F32)],
        [VMEM] * 3 + [SMEM] * 3,
        scratch=[VMEM(row, F32)],
        aliases={0: 0},
    )(acc, zones, same_head, *numbers_in)
    out, kept = call(
        change_kernel,
        [(shape, F32), (rest, F32)],
        [VMEM] * 9 + [SMEM] * 2,
        scratch=[
            VMEM((1024, LANES), F32),
            VMEM((1024, 256), F32),
            VMEM((8, MORE), F32),
            VMEM(row, F32),
            pltpu.SemaphoreType.DMA((8,)),
        ],
        space=pltpu.HBM,
    )(acc, own, total, far_in, cross_in, flip_in, table, zones, same_head, diffusion, courant)
    (out,) = call(
        last_kernel,
        [(shape, F32)],
        [VMEM] * 2 + [SMEM] * 2 + [pltpu.HBM],
        scratch=[VMEM(rest, F32), pltpu.SemaphoreType.DMA((PARTS,))],
        aliases={4: 0},
        space=pltpu.HBM,
    )(kept, same_tail, diffusion, courant, out)
    return out[None]


def solution(mesh):
    placed = (P("grid", "dom", None, None), P("grid", None), P("grid"), P(), P())
    return jax.shard_map(whole, mesh=mesh, in_specs=placed, out_specs=P("grid", "dom", None, None), check_vma=False)
```

profile of v0, /device:TPU:24, one launch (start us, length us, event | category | flops | bytes accessed | tf_op | source)
XLA Modules:
  0.0 41.0 jit_solution(11014338940934012049)
XLA Ops:
  0.0 0.1 collective-permute-start
  0.1 10.3 %collective-permute-start.1 = (f32[2,8,16384]{2,1,0:T(8,128)}, f32[2,8,16384]{2,1,0:T(8,128)S(1)}, u32[]{:S(2)}, u32[]{:S(2)}) collective-permute-start(f32[2,8,16384]{2,1,0:T(8,128)} %bitcast.3), channel_id=1, source_target_pairs={{3,4},{4,3},{7,8},{8,7},{11,12},{12,11},{15,16},{16,15},{19,20},{2... | collective-permute-start | bytes 3145736 | tf_op jit(solution)/shard_map/ppermute | solution.py:430
  11.1 1.2 %copy-done = f32[1,2,8,16384]{3,2,1,0:T(8,128)S(1)} copy-done((f32[1,2,8,16384]{3,2,1,0:T(8,128)S(1)}, f32[1,2,8,16384]{3,2,1,0:T(8,128)}, u32[]{:S(2)}) %copy-start) | copy-done | bytes 1048600
  12.3 3.0 %shard_map.55 = (f32[8,24576]{1,0:T(8,128)S(1)}, f32[8,8192]{1,0:T(8,128)S(1)}, f32[2,8,16384]{2,1,0:T(8,128)S(1)}, f32[16,256]{1,0:T(8,128)S(1)}, f32[8,128]{1,0:T(8,128)S(1)}) custom-call(f32[2,8,16384]{2,1,0:T(8,128)S(1)} %bitcast.4, s32[1,4]{1,0:T(1,128)S(1)} %copy-done.3, f32[6]{0:T(128)S(1)} %copy-done.1, f32[6]{0:T(128)S(1)} %copy-done.2, ...), custom_call_target="tpu_custom_call" | custom-call | flops 1000 | bytes 1000 | tf_op jit(solution)/shard_map/pallas_call | solution.py:431
  15.4 0.7 %collective-permute-start.2 = (f32[8,24576]{1,0:T(8,128)S(1)}, f32[8,24576]{1,0:T(8,128)S(1)}, u32[]{:S(2)}, u32[]{:S(2)}) collective-permute-start(f32[8,24576]{1,0:T(8,128)S(1)} %get-tuple-element.23), channel_id=1, source_target_pairs={{1,2},{2,1},{5,6},{6,5},{9,10},{10,9},{13,14},{14,13},{17,18},{18,... | collective-permute-start | bytes 2359304 | tf_op jit(solution)/shard_map/ppermute | solution.py:437
  16.1 0.7 %collective-permute-start.9 = (f32[8,8192]{1,0:T(8,128)S(1)}, f32[8,8192]{1,0:T(8,128)S(1)}, u32[]{:S(2)}, u32[]{:S(2)}) collective-permute-start(f32[8,8192]{1,0:T(8,128)S(1)} %get-tuple-element.31), channel_id=1, source_target_pairs={{1,2},{2,1},{5,6},{6,5},{9,10},{10,9},{13,14},{14,13},{17,18},{18,... | collective-permute-start | bytes 786440 | tf_op jit(solution)/shard_map/ppermute | solution.py:454
  16.8 0.0 collective-permute-done.k_ref
  16.8 3.2 %shard_map.56 = (f32[2,8,16384]{2,1,0:T(8,128)S(1)}, f32[2,8,16384]{2,1,0:T(8,128)S(1)}, f32[16,256]{1,0:T(8,128)S(1)}, f32[32,256]{1,0:T(8,128)S(1)}, bf16[256,256]{1,0:T(8,128)(2,1)S(1)}) custom-call(f32[2,8,16384]{2,1,0:T(8,128)S(1)} %bitcast.5, f32[2,8,16384]{2,1,0:T(8,128)S(1)} %get-tuple-element.19.z_ref, ...), custom_call_target="tpu_custom_call", output_to_operand_aliasing={{1}: (1, {})} | custom-call | flops 1000 | bytes 1000 | tf_op jit(solution)/shard_map/pallas_call | solution.py:438
  20.0 0.2 collective-permute-start.3
  20.2 2.6 %collective-permute-start.4 = (f32[32,256]{1,0:T(8,128)S(1)}, f32[32,256]{1,0:T(8,128)S(1)}, u32[]{:S(2)}, u32[]{:S(2)}) collective-permute-start(f32[32,256]{1,0:T(8,128)S(1)} %get-tuple-element.25.t_ref), channel_id=1, source_target_pairs={{0,64},{32,96},{64,0},{96,32},{128,192},{160,224},{192,128},{224,1... | collective-permute-start | bytes 98312 | tf_op jit(solution)/shard_map/ppermute | solution.py:447
  22.8 1.1 %collective-permute-done.3.a_ref = f32[32,256]{1,0:T(8,128)S(1)} collective-permute-done((f32[32,256]{1,0:T(8,128)S(1)}, f32[32,256]{1,0:T(8,128)S(1)}, u32[]{:S(2)}, u32[]{:S(2)}) %collective-permute-start.3) | collective-permute-done | bytes 32800 | tf_op jit(solution)/shard_map/ppermute | solution.py:447
  23.9 0.7 %collective-permute-start.5 = (f32[32,256]{1,0:T(8,128)S(1)}, f32[32,256]{1,0:T(8,128)S(1)}, u32[]{:S(2)}, u32[]{:S(2)}) collective-permute-start(f32[32,256]{1,0:T(8,128)S(1)} %get-tuple-element.25.t_ref), channel_id=1, source_target_pairs={{0,96},{32,0},{64,32},{96,64},{128,224},{160,128},{192,160},{224,1... | collective-permute-start | bytes 98312 | tf_op jit(solution)/shard_map/ppermute | solution.py:447
  24.7 1.0 %collective-permute-done.4.b_ref = f32[32,256]{1,0:T(8,128)S(1)} collective-permute-done((f32[32,256]{1,0:T(8,128)S(1)}, f32[32,256]{1,0:T(8,128)S(1)}, u32[]{:S(2)}, u32[]{:S(2)}) %collective-permute-start.4) | collective-permute-done | bytes 32800 | tf_op jit(solution)/shard_map/ppermute | solution.py:447
  25.6 3.4 %collective-permute-done.5.c_ref = f32[32,256]{1,0:T(8,128)S(1)} collective-permute-done((f32[32,256]{1,0:T(8,128)S(1)}, f32[32,256]{1,0:T(8,128)S(1)}, u32[]{:S(2)}, u32[]{:S(2)}) %collective-permute-start.5) | collective-permute-done | bytes 32800 | tf_op jit(solution)/shard_map/ppermute | solution.py:447
  29.1 0.1 collective-permute-start.6
  29.2 5.1 %collective-permute-start.7 = (f32[16,256]{1,0:T(8,128)S(1)}, f32[16,256]{1,0:T(8,128)S(1)}, u32[]{:S(2)}, u32[]{:S(2)}) collective-permute-start(f32[16,256]{1,0:T(8,128)S(1)} %get-tuple-element.28), channel_id=1, source_target_pairs={{1,130},{2,129},{5,134},{6,133},{9,138},{10,137},{13,142},{14,141}... | collective-permute-start | bytes 49160 | tf_op jit(solution)/shard_map/ppermute | solution.py:452
  34.2 0.0 collective-permute-done.2.same_ref.head_ref
  34.2 0.2 collective-permute-start.8
  34.5 0.0 collective-permute-done.1.zones_ref
  34.5 1.7 %shard_map.57.acc_ref = f32[2,8,16384]{2,1,0:T(8,128)S(1)} custom-call(f32[2,8,16384]{2,1,0:T(8,128)S(1)} %get-tuple-element.22.acc_ref, f32[2,8,16384]{2,1,0:T(8,128)S(1)} %collective-permute-done.1.zones_ref, f32[8,24576]{1,0:T(8,128)S(1)} %collective-permute-done.2.same_ref.head_ref, s32[1,4]{1,0:T(1,128)S(1)} %copy-done.3, ...), custom_call_target="tpu_custom_call", output_to_operand_aliasing={{}: (0, {})} | custom-call | flops 1000 | bytes 1000 | tf_op jit(solution)/shard_map/pallas_call | solution.py:455
  36.2 0.0 collective-permute-done.7.cross_ref
  36.2 1.8 %collective-permute-done.8.flip_ref = f32[16,256]{1,0:T(8,128)S(1)} collective-permute-done((f32[16,256]{1,0:T(8,128)S(1)}, f32[16,256]{1,0:T(8,128)S(1)}, u32[]{:S(2)}, u32[]{:S(2)}) %collective-permute-start.8) | collective-permute-done | bytes 16416 | tf_op jit(solution)/shard_map/ppermute | solution.py:453
  38.0 2.4 %shard_map.59 = (f32[2,8,16384]{2,1,0:T(8,128)}, f32[8,8192]{1,0:T(8,128)S(1)}) custom-call(f32[2,8,16384]{2,1,0:T(8,128)S(1)} %shard_map.57.acc_ref, f32[16,256]{1,0:T(8,128)S(1)} %get-tuple-element.24.own_ref, f32[16,256]{1,0:T(8,128)S(1)} %get-tuple-element.26.sum_ref, f32[32,256]{1,0:T(8,128)S(1)} %collective-permute-done.6.far_ref, ...), custom_call_target="tpu_custom_call" | custom-call | flops 1000 | bytes 1000 | tf_op jit(solution)/shard_map/pallas_call | solution.py:462
  40.4 0.6 %shard_map.60 = f32[2,8,16384]{2,1,0:T(8,128)} custom-call(f32[8,8192]{1,0:T(8,128)S(1)} %get-tuple-element.30.rest_ref, f32[8,8192]{1,0:T(8,128)S(1)} %collective-permute-done.9.tail_ref, f32[6]{0:T(128)S(1)} %copy-done.1, f32[6]{0:T(128)S(1)} %copy-done.2, f32[2,8,16384]{2,1,0:T(8,128)} %get-tuple-element.32.old_ref), custom_call_target="tpu_custom_call", output_to_operand_aliasing={{}: (4, {})} | custom-call | flops 1000 | bytes 1000 | tf_op jit(solution)/shard_map/pallas_call | solution.py:475
  (10 shorter events, 0.0 us)
Async XLA Ops:
  0.0 11.1 %copy-start.1 = (f32[6]{0:T(128)S(1)}, f32[6]{0:T(128)}, u32[]{:S(2)}) copy-start(f32[6]{0:T(128)} %diff_ref.9) | copy-start | bytes 76
  0.0 11.1 %copy-start.2 = (f32[6]{0:T(128)S(1)}, f32[6]{0:T(128)}, u32[]{:S(2)}) copy-start(f32[6]{0:T(128)} %cour_ref.9) | copy-start | bytes 76
  0.0 11.1 %copy-start.3 = (s32[1,4]{1,0:T(1,128)S(1)}, s32[1,4]{1,0:T(1,128)}, u32[]{:S(2)}) copy-start(s32[1,4]{1,0:T(1,128)} %level_ref.5) | copy-start | bytes 52
  0.0 16.8 %collective-permute-start = (f32[2,8,16384]{2,1,0:T(8,128)}, f32[2,8,16384]{2,1,0:T(8,128)S(1)}, u32[]{:S(2)}, u32[]{:S(2)}) collective-permute-start(f32[2,8,16384]{2,1,0:T(8,128)} %bitcast.2), channel_id=1, source_target_pairs={{0,1},{1,0},{2,3},{3,2},{4,5},{5,4},{6,7},{7,6},{8,9},{9,8},{10,11... | collective-permute-start | bytes 3145736 | tf_op jit(solution)/shard_map/ppermute | solution.py:429
  0.1 34.4 %collective-permute-start.1 = (f32[2,8,16384]{2,1,0:T(8,128)}, f32[2,8,16384]{2,1,0:T(8,128)S(1)}, u32[]{:S(2)}, u32[]{:S(2)}) collective-permute-start(f32[2,8,16384]{2,1,0:T(8,128)} %bitcast.3), channel_id=1, source_target_pairs={{3,4},{4,3},{7,8},{8,7},{11,12},{12,11},{15,16},{16,15},{19,20},{2... | collective-permute-start | bytes 3145736 | tf_op jit(solution)/shard_map/ppermute | solution.py:430
  11.1 1.2 %copy-start = (f32[1,2,8,16384]{3,2,1,0:T(8,128)S(1)}, f32[1,2,8,16384]{3,2,1,0:T(8,128)}, u32[]{:S(2)}) copy-start(f32[1,2,8,16384]{3,2,1,0:T(8,128)} %param.5) | copy-start | bytes 3145732
  15.4 18.9 %collective-permute-start.2 = (f32[8,24576]{1,0:T(8,128)S(1)}, f32[8,24576]{1,0:T(8,128)S(1)}, u32[]{:S(2)}, u32[]{:S(2)}) collective-permute-start(f32[8,24576]{1,0:T(8,128)S(1)} %get-tuple-element.23), channel_id=1, source_target_pairs={{1,2},{2,1},{5,6},{6,5},{9,10},{10,9},{13,14},{14,13},{17,18},{18,... | collective-permute-start | bytes 2359304 | tf_op jit(solution)/shard_map/ppermute | solution.py:437
  16.1 24.3 %collective-permute-start.9 = (f32[8,8192]{1,0:T(8,128)S(1)}, f32[8,8192]{1,0:T(8,128)S(1)}, u32[]{:S(2)}, u32[]{:S(2)}) collective-permute-start(f32[8,8192]{1,0:T(8,128)S(1)} %get-tuple-element.31), channel_id=1, source_target_pairs={{1,2},{2,1},{5,6},{6,5},{9,10},{10,9},{13,14},{14,13},{17,18},{18,... | collective-permute-start | bytes 786440 | tf_op jit(solution)/shard_map/ppermute | solution.py:454
  20.0 3.9 %collective-permute-start.3 = (f32[32,256]{1,0:T(8,128)S(1)}, f32[32,256]{1,0:T(8,128)S(1)}, u32[]{:S(2)}, u32[]{:S(2)}) collective-permute-start(f32[32,256]{1,0:T(8,128)S(1)} %get-tuple-element.25.t_ref), channel_id=1, source_target_pairs={{0,32},{32,64},{64,96},{96,0},{128,160},{160,192},{192,224},{224,1... | collective-permute-start | bytes 98312 | tf_op jit(solution)/shard_map/ppermute | solution.py:447
  20.2 5.4 %collective-permute-start.4 = (f32[32,256]{1,0:T(8,128)S(1)}, f32[32,256]{1,0:T(8,128)S(1)}, u32[]{:S(2)}, u32[]{:S(2)}) collective-permute-start(f32[32,256]{1,0:T(8,128)S(1)} %get-tuple-element.25.t_ref), channel_id=1, source_target_pairs={{0,64},{32,96},{64,0},{96,32},{128,192},{160,224},{192,128},{224,1... | collective-permute-start | bytes 98312 | tf_op jit(solution)/shard_map/ppermute | solution.py:447
  23.9 5.1 %collective-permute-start.5 = (f32[32,256]{1,0:T(8,128)S(1)}, f32[32,256]{1,0:T(8,128)S(1)}, u32[]{:S(2)}, u32[]{:S(2)}) collective-permute-start(f32[32,256]{1,0:T(8,128)S(1)} %get-tuple-element.25.t_ref), channel_id=1, source_target_pairs={{0,96},{32,0},{64,32},{96,64},{128,224},{160,128},{192,160},{224,1... | collective-permute-start | bytes 98312 | tf_op jit(solution)/shard_map/ppermute | solution.py:447
  29.1 8.9 %collective-permute-start.6 = (f32[32,256]{1,0:T(8,128)S(1)}, f32[32,256]{1,0:T(8,128)S(1)}, u32[]{:S(2)}, u32[]{:S(2)}) collective-permute-start(f32[32,256]{1,0:T(8,128)S(1)} %get-tuple-element.27), channel_id=1, source_target_pairs={{1,2},{2,1},{5,6},{6,5},{9,10},{10,9},{13,14},{14,13},{17,18},{18,... | collective-permute-start | bytes 98312 | tf_op jit(solution)/shard_map/ppermute | solution.py:451
  29.2 7.0 %collective-permute-start.7 = (f32[16,256]{1,0:T(8,128)S(1)}, f32[16,256]{1,0:T(8,128)S(1)}, u32[]{:S(2)}, u32[]{:S(2)}) collective-permute-start(f32[16,256]{1,0:T(8,128)S(1)} %get-tuple-element.28), channel_id=1, source_target_pairs={{1,130},{2,129},{5,134},{6,133},{9,138},{10,137},{13,142},{14,141}... | collective-permute-start | bytes 49160 | tf_op jit(solution)/shard_map/ppermute | solution.py:452
  34.2 3.7 %collective-permute-start.8 = (f32[16,256]{1,0:T(8,128)S(1)}, f32[16,256]{1,0:T(8,128)S(1)}, u32[]{:S(2)}, u32[]{:S(2)}) collective-permute-start(f32[16,256]{1,0:T(8,128)S(1)} %get-tuple-element.26.sum_ref), channel_id=1, source_target_pairs={{0,128},{32,160},{64,192},{96,224},{128,0},{160,32},{192,64},{224,... | collective-permute-start | bytes 49160 | tf_op jit(solution)/shard_map/ppermute | solution.py:453
where the time goes:
time: 41.2 us; the launch traced here: 41 us
  starting transfers between devices  20.8 us (50%)
  Pallas kernels  10.9 us (26%)
  waiting for transfers between devices  7.29 us (18%)
  local copies, waits for them, and re-layouts  1.23 us (3%)
  between operations  0.78 us (2%)
    ppermute x1, starting transfers between devices, whole(): zones = lax.ppermute(u, 'dom', pairs_zone)  10.3 us
    ppermute x3, waiting for transfers between devices, whole(): turned.append(lax.ppermute(t, 'grid', pairs))  5.48 us
    ppermute x1, starting transfers between devices, whole(): cross_in = lax.ppermute(cross, ('grid', 'dom'), pairs_cross)  5.08 us
    ppermute x3, starting transfers between devices, whole(): turned.append(lax.ppermute(t, 'grid', pairs))  3.58 us
    pallas_call x1, Pallas kernels, whole(): call(second_kernel, [(shape, F32), (shape, F32), (points, F32), ((32, 256...  3.18 us
    pallas_call x1, Pallas kernels, whole(): call(first_kernel, [((8, COLS + MORE), F32), (rest, F32), (shape, F32), (...  3.04 us
    pallas_call x1, Pallas kernels, whole(): call(change_kernel, [(shape, F32), (rest, F32)], [VMEM] * 9 + [SMEM] * 2,...  2.39 us
    ppermute x1, waiting for transfers between devices, whole(): flip_in = lax.ppermute(total, 'grid', pairs_flip)  1.79 us
  transfers between devices with their start and end apart: 10, of which 4 were waited for; matrix products, arithmetic and copies ran while one was open for 0% of the time, Pallas kernels for 25%

commit v1 on v0

--- a/solution.py
+++ b/solution.py
@@ -335,7 +335,12 @@
     reach = 8 - jnp.minimum(gap, 32 - gap)
     point = (source % 8 == 0) & (source < 32) & (reach > 0)
     table = jnp.where(point, (near * reach).astype(F32) * (1.0 / 32.0), 0.0).astype(BF16)
-    wide_ref[...] = exact_dot(chunks_ref[...], table, False)
+    x = chunks_ref[...]
+    high = x.astype(BF16)
+    low = (x - high.astype(F32)).astype(BF16)
+    dims = (((1,), (0,)), ((), ()))
+    parts = lax.dot_general(jnp.concatenate([high, low], axis=0), table, dims, preferred_element_type=F32)
+    wide_ref[...] = parts[:1024] + parts[1024:]
     copies = []
     for i2 in range(4):
         for c in range(4):

time: 41.2 us -> 40.9 us (level)
  no operation moved by 1% of the time
where the time goes in v1:
time: 40.9 us; the launch traced here: 40.7 us
  starting transfers between devices  20.8 us (51%)
  Pallas kernels  10.6 us (26%)
  waiting for transfers between devices  7.29 us (18%)
  local copies, waits for them, and re-layouts  1.23 us (3%)
  between operations  0.78 us (2%)
    ppermute x1, starting transfers between devices, whole(): zones = lax.ppermute(u, 'dom', pairs_zone)  10.3 us
    ppermute x3, waiting for transfers between devices, whole(): turned.append(lax.ppermute(t, 'grid', pairs))  5.48 us
    ppermute x1, starting transfers between devices, whole(): cross_in = lax.ppermute(cross, ('grid', 'dom'), pairs_cross)  5.08 us
    ppermute x3, starting transfers between devices, whole(): turned.append(lax.ppermute(t, 'grid', pairs))  3.58 us
    pallas_call x1, Pallas kernels, whole(): call(second_kernel, [(shape, F32), (shape, F32), (points, F32), ((32, 256...  3.18 us
    pallas_call x1, Pallas kernels, whole(): call(first_kernel, [((8, COLS + MORE), F32), (rest, F32), (shape, F32), (...  3.04 us
    pallas_call x1, Pallas kernels, whole(): call(change_kernel, [(shape, F32), (rest, F32)], [VMEM] * 9 + [SMEM] * 2,...  2.1 us
    ppermute x1, waiting for transfers between devices, whole(): flip_in = lax.ppermute(total, 'grid', pairs_flip)  1.79 us
  transfers between devices with their start and end apart: 10, of which 4 were waited for; matrix products, arithmetic and copies ran while one was open for 0% of the time, Pallas kernels for 25%

profile of v1, /device:TPU:24, one launch (start us, length us, event | category | flops | bytes accessed | tf_op | source)
XLA Modules:
  0.0 40.7 jit_solution(8067940165215383023)
XLA Ops:
  0.0 0.1 collective-permute-start
  0.1 10.3 %collective-permute-start.1 = (f32[2,8,16384]{2,1,0:T(8,128)}, f32[2,8,16384]{2,1,0:T(8,128)S(1)}, u32[]{:S(2)}, u32[]{:S(2)}) collective-permute-start(f32[2,8,16384]{2,1,0:T(8,128)} %bitcast.3), channel_id=1, source_target_pairs={{3,4},{4,3},{7,8},{8,7},{11,12},{12,11},{15,16},{16,15},{19,20},{2... | collective-permute-start | bytes 3145736 | tf_op jit(solution)/shard_map/ppermute | solution.py:435
  11.1 1.2 %copy-done = f32[1,2,8,16384]{3,2,1,0:T(8,128)S(1)} copy-done((f32[1,2,8,16384]{3,2,1,0:T(8,128)S(1)}, f32[1,2,8,16384]{3,2,1,0:T(8,128)}, u32[]{:S(2)}) %copy-start) | copy-done | bytes 1048600
  12.3 3.0 %shard_map.55 = (f32[8,24576]{1,0:T(8,128)S(1)}, f32[8,8192]{1,0:T(8,128)S(1)}, f32[2,8,16384]{2,1,0:T(8,128)S(1)}, f32[16,256]{1,0:T(8,128)S(1)}, f32[8,128]{1,0:T(8,128)S(1)}) custom-call(f32[2,8,16384]{2,1,0:T(8,128)S(1)} %bitcast.4, s32[1,4]{1,0:T(1,128)S(1)} %copy-done.3, f32[6]{0:T(128)S(1)} %copy-done.1, f32[6]{0:T(128)S(1)} %copy-done.2, ...), custom_call_target="tpu_custom_call" | custom-call | flops 1000 | bytes 1000 | tf_op jit(solution)/shard_map/pallas_call | solution.py:436
  15.4 0.7 %collective-permute-start.2 = (f32[8,24576]{1,0:T(8,128)S(1)}, f32[8,24576]{1,0:T(8,128)S(1)}, u32[]{:S(2)}, u32[]{:S(2)}) collective-permute-start(f32[8,24576]{1,0:T(8,128)S(1)} %get-tuple-element.23), channel_id=1, source_target_pairs={{1,2},{2,1},{5,6},{6,5},{9,10},{10,9},{13,14},{14,13},{17,18},{18,... | collective-permute-start | bytes 2359304 | tf_op jit(solution)/shard_map/ppermute | solution.py:442
  16.1 0.7 %collective-permute-start.9 = (f32[8,8192]{1,0:T(8,128)S(1)}, f32[8,8192]{1,0:T(8,128)S(1)}, u32[]{:S(2)}, u32[]{:S(2)}) collective-permute-start(f32[8,8192]{1,0:T(8,128)S(1)} %get-tuple-element.31), channel_id=1, source_target_pairs={{1,2},{2,1},{5,6},{6,5},{9,10},{10,9},{13,14},{14,13},{17,18},{18,... | collective-permute-start | bytes 786440 | tf_op jit(solution)/shard_map/ppermute | solution.py:459
  16.8 0.0 collective-permute-done.k_ref
  16.8 3.2 %shard_map.56 = (f32[2,8,16384]{2,1,0:T(8,128)S(1)}, f32[2,8,16384]{2,1,0:T(8,128)S(1)}, f32[16,256]{1,0:T(8,128)S(1)}, f32[32,256]{1,0:T(8,128)S(1)}, bf16[256,256]{1,0:T(8,128)(2,1)S(1)}) custom-call(f32[2,8,16384]{2,1,0:T(8,128)S(1)} %bitcast.5, f32[2,8,16384]{2,1,0:T(8,128)S(1)} %get-tuple-element.19.z_ref, ...), custom_call_target="tpu_custom_call", output_to_operand_aliasing={{1}: (1, {})} | custom-call | flops 1000 | bytes 1000 | tf_op jit(solution)/shard_map/pallas_call | solution.py:443
  20.0 0.2 collective-permute-start.3
  20.2 2.6 %collective-permute-start.4 = (f32[32,256]{1,0:T(8,128)S(1)}, f32[32,256]{1,0:T(8,128)S(1)}, u32[]{:S(2)}, u32[]{:S(2)}) collective-permute-start(f32[32,256]{1,0:T(8,128)S(1)} %get-tuple-element.25.t_ref), channel_id=1, source_target_pairs={{0,64},{32,96},{64,0},{96,32},{128,192},{160,224},{192,128},{224,1... | collective-permute-start | bytes 98312 | tf_op jit(solution)/shard_map/ppermute | solution.py:452
  22.8 1.1 %collective-permute-done.3.a_ref = f32[32,256]{1,0:T(8,128)S(1)} collective-permute-done((f32[32,256]{1,0:T(8,128)S(1)}, f32[32,256]{1,0:T(8,128)S(1)}, u32[]{:S(2)}, u32[]{:S(2)}) %collective-permute-start.3) | collective-permute-done | bytes 32800 | tf_op jit(solution)/shard_map/ppermute | solution.py:452
  23.9 0.7 %collective-permute-start.5 = (f32[32,256]{1,0:T(8,128)S(1)}, f32[32,256]{1,0:T(8,128)S(1)}, u32[]{:S(2)}, u32[]{:S(2)}) collective-permute-start(f32[32,256]{1,0:T(8,128)S(1)} %get-tuple-element.25.t_ref), channel_id=1, source_target_pairs={{0,96},{32,0},{64,32},{96,64},{128,224},{160,128},{192,160},{224,1... | collective-permute-start | bytes 98312 | tf_op jit(solution)/shard_map/ppermute | solution.py:452
  24.7 1.0 %collective-permute-done.4.b_ref = f32[32,256]{1,0:T(8,128)S(1)} collective-permute-done((f32[32,256]{1,0:T(8,128)S(1)}, f32[32,256]{1,0:T(8,128)S(1)}, u32[]{:S(2)}, u32[]{:S(2)}) %collective-permute-start.4) | collective-permute-done | bytes 32800 | tf_op jit(solution)/shard_map/ppermute | solution.py:452
  25.6 3.4 %collective-permute-done.5.c_ref = f32[32,256]{1,0:T(8,128)S(1)} collective-permute-done((f32[32,256]{1,0:T(8,128)S(1)}, f32[32,256]{1,0:T(8,128)S(1)}, u32[]{:S(2)}, u32[]{:S(2)}) %collective-permute-start.5) | collective-permute-done | bytes 32800 | tf_op jit(solution)/shard_map/ppermute | solution.py:452
  29.1 0.1 collective-permute-start.6
  29.2 5.1 %collective-permute-start.7 = (f32[16,256]{1,0:T(8,128)S(1)}, f32[16,256]{1,0:T(8,128)S(1)}, u32[]{:S(2)}, u32[]{:S(2)}) collective-permute-start(f32[16,256]{1,0:T(8,128)S(1)} %get-tuple-element.28), channel_id=1, source_target_pairs={{1,130},{2,129},{5,134},{6,133},{9,138},{10,137},{13,142},{14,141}... | collective-permute-start | bytes 49160 | tf_op jit(solution)/shard_map/ppermute | solution.py:457
  34.2 0.0 collective-permute-done.2.same_ref.head_ref
  34.2 0.2 collective-permute-start.8
  34.5 0.0 collective-permute-done.1.zones_ref
  34.5 1.7 %shard_map.57.acc_ref = f32[2,8,16384]{2,1,0:T(8,128)S(1)} custom-call(f32[2,8,16384]{2,1,0:T(8,128)S(1)} %get-tuple-element.22.acc_ref, f32[2,8,16384]{2,1,0:T(8,128)S(1)} %collective-permute-done.1.zones_ref, f32[8,24576]{1,0:T(8,128)S(1)} %collective-permute-done.2.same_ref.head_ref, s32[1,4]{1,0:T(1,128)S(1)} %copy-done.3, ...), custom_call_target="tpu_custom_call", output_to_operand_aliasing={{}: (0, {})} | custom-call | flops 1000 | bytes 1000 | tf_op jit(solution)/shard_map/pallas_call | solution.py:460
  36.2 0.0 collective-permute-done.7.cross_ref
  36.2 1.8 %collective-permute-done.8.flip_ref = f32[16,256]{1,0:T(8,128)S(1)} collective-permute-done((f32[16,256]{1,0:T(8,128)S(1)}, f32[16,256]{1,0:T(8,128)S(1)}, u32[]{:S(2)}, u32[]{:S(2)}) %collective-permute-start.8) | collective-permute-done | bytes 16416 | tf_op jit(solution)/shard_map/ppermute | solution.py:458
  38.0 2.1 %shard_map.59 = (f32[2,8,16384]{2,1,0:T(8,128)}, f32[8,8192]{1,0:T(8,128)S(1)}) custom-call(f32[2,8,16384]{2,1,0:T(8,128)S(1)} %shard_map.57.acc_ref, f32[16,256]{1,0:T(8,128)S(1)} %get-tuple-element.24.own_ref, f32[16,256]{1,0:T(8,128)S(1)} %get-tuple-element.26.sum_ref, f32[32,256]{1,0:T(8,128)S(1)} %collective-permute-done.6.far_ref, ...), custom_call_target="tpu_custom_call" | custom-call | flops 1000 | bytes 1000 | tf_op jit(solution)/shard_map/pallas_call | solution.py:467
  40.1 0.6 %shard_map.60 = f32[2,8,16384]{2,1,0:T(8,128)} custom-call(f32[8,8192]{1,0:T(8,128)S(1)} %get-tuple-element.30.rest_ref, f32[8,8192]{1,0:T(8,128)S(1)} %collective-permute-done.9.tail_ref, f32[6]{0:T(128)S(1)} %copy-done.1, f32[6]{0:T(128)S(1)} %copy-done.2, f32[2,8,16384]{2,1,0:T(8,128)} %get-tuple-element.32.old_ref), custom_call_target="tpu_custom_call", output_to_operand_aliasing={{}: (4, {})} | custom-call | flops 1000 | bytes 1000 | tf_op jit(solution)/shard_map/pallas_call | solution.py:480
  (10 shorter events, 0.0 us)
Async XLA Ops:
  0.0 11.1 %copy-start.1 = (f32[6]{0:T(128)S(1)}, f32[6]{0:T(128)}, u32[]{:S(2)}) copy-start(f32[6]{0:T(128)} %diff_ref.9) | copy-start | bytes 76
  0.0 11.1 %copy-start.2 = (f32[6]{0:T(128)S(1)}, f32[6]{0:T(128)}, u32[]{:S(2)}) copy-start(f32[6]{0:T(128)} %cour_ref.9) | copy-start | bytes 76
  0.0 11.1 %copy-start.3 = (s32[1,4]{1,0:T(1,128)S(1)}, s32[1,4]{1,0:T(1,128)}, u32[]{:S(2)}) copy-start(s32[1,4]{1,0:T(1,128)} %level_ref.5) | copy-start | bytes 52
  0.0 16.8 %collective-permute-start = (f32[2,8,16384]{2,1,0:T(8,128)}, f32[2,8,16384]{2,1,0:T(8,128)S(1)}, u32[]{:S(2)}, u32[]{:S(2)}) collective-permute-start(f32[2,8,16384]{2,1,0:T(8,128)} %bitcast.2), channel_id=1, source_target_pairs={{0,1},{1,0},{2,3},{3,2},{4,5},{5,4},{6,7},{7,6},{8,9},{9,8},{10,11... | collective-permute-start | bytes 3145736 | tf_op jit(solution)/shard_map/ppermute | solution.py:434
  0.1 34.4 %collective-permute-start.1 = (f32[2,8,16384]{2,1,0:T(8,128)}, f32[2,8,16384]{2,1,0:T(8,128)S(1)}, u32[]{:S(2)}, u32[]{:S(2)}) collective-permute-start(f32[2,8,16384]{2,1,0:T(8,128)} %bitcast.3), channel_id=1, source_target_pairs={{3,4},{4,3},{7,8},{8,7},{11,12},{12,11},{15,16},{16,15},{19,20},{2... | collective-permute-start | bytes 3145736 | tf_op jit(solution)/shard_map/ppermute | solution.py:435
  11.1 1.2 %copy-start = (f32[1,2,8,16384]{3,2,1,0:T(8,128)S(1)}, f32[1,2,8,16384]{3,2,1,0:T(8,128)}, u32[]{:S(2)}) copy-start(f32[1,2,8,16384]{3,2,1,0:T(8,128)} %param.5) | copy-start | bytes 3145732
  15.4 18.9 %collective-permute-start.2 = (f32[8,24576]{1,0:T(8,128)S(1)}, f32[8,24576]{1,0:T(8,128)S(1)}, u32[]{:S(2)}, u32[]{:S(2)}) collective-permute-start(f32[8,24576]{1,0:T(8,128)S(1)} %get-tuple-element.23), channel_id=1, source_target_pairs={{1,2},{2,1},{5,6},{6,5},{9,10},{10,9},{13,14},{14,13},{17,18},{18,... | collective-permute-start | bytes 2359304 | tf_op jit(solution)/shard_map/ppermute | solution.py:442
  16.1 24.0 %collective-permute-start.9 = (f32[8,8192]{1,0:T(8,128)S(1)}, f32[8,8192]{1,0:T(8,128)S(1)}, u32[]{:S(2)}, u32[]{:S(2)}) collective-permute-start(f32[8,8192]{1,0:T(8,128)S(1)} %get-tuple-element.31), channel_id=1, source_target_pairs={{1,2},{2,1},{5,6},{6,5},{9,10},{10,9},{13,14},{14,13},{17,18},{18,... | collective-permute-start | bytes 786440 | tf_op jit(solution)/shard_map/ppermute | solution.py:459
  20.0 3.9 %collective-permute-start.3 = (f32[32,256]{1,0:T(8,128)S(1)}, f32[32,256]{1,0:T(8,128)S(1)}, u32[]{:S(2)}, u32[]{:S(2)}) collective-permute-start(f32[32,256]{1,0:T(8,128)S(1)} %get-tuple-element.25.t_ref), channel_id=1, source_target_pairs={{0,32},{32,64},{64,96},{96,0},{128,160},{160,192},{192,224},{224,1... | collective-permute-start | bytes 98312 | tf_op jit(solution)/shard_map/ppermute | solution.py:452
  20.2 5.4 %collective-permute-start.4 = (f32[32,256]{1,0:T(8,128)S(1)}, f32[32,256]{1,0:T(8,128)S(1)}, u32[]{:S(2)}, u32[]{:S(2)}) collective-permute-start(f32[32,256]{1,0:T(8,128)S(1)} %get-tuple-element.25.t_ref), channel_id=1, source_target_pairs={{0,64},{32,96},{64,0},{96,32},{128,192},{160,224},{192,128},{224,1... | collective-permute-start | bytes 98312 | tf_op jit(solution)/shard_map/ppermute | solution.py:452
  23.9 5.1 %collective-permute-start.5 = (f32[32,256]{1,0:T(8,128)S(1)}, f32[32,256]{1,0:T(8,128)S(1)}, u32[]{:S(2)}, u32[]{:S(2)}) collective-permute-start(f32[32,256]{1,0:T(8,128)S(1)} %get-tuple-element.25.t_ref), channel_id=1, source_target_pairs={{0,96},{32,0},{64,32},{96,64},{128,224},{160,128},{192,160},{224,1... | collective-permute-start | bytes 98312 | tf_op jit(solution)/shard_map/ppermute | solution.py:452
  29.1 8.9 %collective-permute-start.6 = (f32[32,256]{1,0:T(8,128)S(1)}, f32[32,256]{1,0:T(8,128)S(1)}, u32[]{:S(2)}, u32[]{:S(2)}) collective-permute-start(f32[32,256]{1,0:T(8,128)S(1)} %get-tuple-element.27), channel_id=1, source_target_pairs={{1,2},{2,1},{5,6},{6,5},{9,10},{10,9},{13,14},{14,13},{17,18},{18,... | collective-permute-start | bytes 98312 | tf_op jit(solution)/shard_map/ppermute | solution.py:456
  29.2 7.0 %collective-permute-start.7 = (f32[16,256]{1,0:T(8,128)S(1)}, f32[16,256]{1,0:T(8,128)S(1)}, u32[]{:S(2)}, u32[]{:S(2)}) collective-permute-start(f32[16,256]{1,0:T(8,128)S(1)} %get-tuple-element.28), channel_id=1, source_target_pairs={{1,130},{2,129},{5,134},{6,133},{9,138},{10,137},{13,142},{14,141}... | collective-permute-start | bytes 49160 | tf_op jit(solution)/shard_map/ppermute | solution.py:457
  34.2 3.7 %collective-permute-start.8 = (f32[16,256]{1,0:T(8,128)S(1)}, f32[16,256]{1,0:T(8,128)S(1)}, u32[]{:S(2)}, u32[]{:S(2)}) collective-permute-start(f32[16,256]{1,0:T(8,128)S(1)} %get-tuple-element.26.sum_ref), channel_id=1, source_target_pairs={{0,128},{32,160},{64,192},{96,224},{128,0},{160,32},{192,64},{224,... | collective-permute-start | bytes 49160 | tf_op jit(solution)/shard_map/ppermute | solution.py:458
